TPU v7x, 128 devices: a whole 4x4x4 slice. The times are simulated.
128 devices in a mesh: dp: 4 (over y), ctx: 32 (over z, x, core).
Axes of the slice: x: 4, y: 4, z: 4, core: 2. Of those that a mesh axis runs over, the one named last changes fastest.
Arguments:
- projected: bfloat16 [4, 4096, 3, 8192], P('dp', 'ctx'), may hold values from -6 to 6
- short_filter: float32 [3, 7, 8192], replicated, may hold values from -2.4 to 2.4
- residues: float32 [512, 16], replicated, may hold values from -0.06 to 0.06
- decay_rates: float32 [512, 16], replicated, may hold values from 2.4414063e-05 to 0.03125
- skip_gain: float32 [8192], replicated, may hold values from 0.5 to 1.5
- cotangent: bfloat16 [4, 4096, 8192], P('dp', 'ctx'), may hold values from -6 to 6
Outputs:
- output: bfloat16 [4, 4096, 8192], P('dp', 'ctx')
- grad_projected: bfloat16 [4, 4096, 3, 8192], P('dp', 'ctx')
- grad_short: float32 [3, 7, 8192], replicated
- grad_skip: float32 [8192], replicated
All inputs are finite; a program needn't handle non-finite values.
Results may differ from a plain program's by a relative error of at most 0.001.
Values may be sent and summed in bfloat16 or wider, within the bound.
A program may use at most 320 MiB of HBM per device.

v0:
```python
import jax
import jax.numpy as jnp
from jax import lax
from jax.sharding import PartitionSpec as P

BLK = 64
HIGHEST = lax.Precision.HIGHEST


def passed_along(value, axis, steps):
    count = lax.axis_size(axis)
    first, last = (max(0, -steps), min(count, count - steps))
    return lax.ppermute(value, axis, [(source, source + steps) for source in range(first, last)])


def edge_tables(residues, decay_rates, span):
    offsets = jnp.arange(span).astype(jnp.float32)
    carry_fwd = residues[:, None, :] * jnp.exp(
        -decay_rates[:, None, :] * (offsets[None, :, None] + 1.0)
    )
    carry_bwd = residues[:, None, :] * jnp.exp(
        -decay_rates[:, None, :] * (span - offsets)[None, :, None]
    )
    decay_factor = jnp.exp(-decay_rates * span)
    return (carry_fwd, carry_bwd, decay_factor)


def block_tables(residues, decay_rates, block_rows):
    offsets = jnp.arange(block_rows).astype(jnp.float32)
    powers = jnp.exp(-decay_rates[:, :, None] * offsets[None, None, :])
    lag_filter = jnp.sum(residues[:, :, None] * powers, axis=1)
    lag_index = jnp.arange(block_rows)[:, None] - jnp.arange(block_rows)[None, :]
    toeplitz = jnp.where(lag_index >= 0, lag_filter[:, jnp.maximum(lag_index, 0)], 0.0)
    carry_fwd, carry_bwd, decay_factor = edge_tables(residues, decay_rates, block_rows)
    return (toeplitz, powers[:, :, ::-1], powers, carry_fwd, carry_bwd, decay_factor)


def forward_local(inputs, tables):
    toeplitz, end_weights, start_weights, carry_fwd, carry_bwd, decay_factor = tables
    local_out = jnp.einsum("gts,bkswg->bktwg", toeplitz, inputs, precision=HIGHEST)
    block_ends = jnp.einsum("gns,bkswg->bknwg", end_weights, inputs, precision=HIGHEST)
    factor = decay_factor.T[:, None, :]

    def forward_advance(carried, block_term):
        return (factor * carried + block_term, carried)

    final_state, entering = lax.scan(
        forward_advance, jnp.zeros_like(block_ends[:, 0]), jnp.moveaxis(block_ends, 1, 0)
    )
    entering = jnp.moveaxis(entering, 0, 1)
    local_out = local_out + jnp.einsum("gjn,bknwg->bkjwg", carry_fwd, entering, precision=HIGHEST)
    return (local_out, final_state)


def backward_local(grads, tables):
    toeplitz, end_weights, start_weights, carry_fwd, carry_bwd, decay_factor = tables
    local_grad = jnp.einsum("gts,bktwg->bkswg", toeplitz, grads, precision=HIGHEST)
    block_starts = jnp.einsum("gnt,bktwg->bknwg", start_weights, grads, precision=HIGHEST)
    factor = decay_factor.T[:, None, :]

    def backward_advance(carried, block_term):
        return (factor * carried + block_term, carried)

    final_adjoint, following = lax.scan(
        backward_advance,
        jnp.zeros_like(block_starts[:, 0]),
        jnp.moveaxis(block_starts, 1, 0),
        reverse=True,
    )
    following = jnp.moveaxis(following, 0, 1)
    local_grad = local_grad + jnp.einsum(
        "gsn,bknwg->bkswg", carry_bwd, following, precision=HIGHEST
    )
    return (local_grad, final_adjoint)


def short_conv(padded, short_filter, count):
    tap_count = short_filter.shape[1]
    total = jnp.zeros((padded.shape[0], count) + padded.shape[2:], jnp.float32)
    for offset in range(tap_count):
        begin = tap_count - 1 - offset
        total = total + short_filter[:, offset, :] * padded[:, begin : begin + count].astype(
            jnp.float32
        )
    return total


def short_conv_grad(ahead, short_filter, count):
    tap_count = short_filter.shape[1]
    total = jnp.zeros((ahead.shape[0], count) + ahead.shape[2:], jnp.float32)
    for offset in range(tap_count):
        total = total + short_filter[:, offset, :] * ahead[:, offset : offset + count]
    return total


def filter_grad(grad_mixed, padded, tap_count, count):
    products = jnp.stack(
        [
            grad_mixed
            * padded[:, tap_count - 1 - offset : tap_count - 1 - offset + count].astype(jnp.float32)
            for offset in range(tap_count)
        ],
        axis=3,
    )
    return jnp.sum(products, axis=(0, 1))


def chains(local_end, local_adjoint, factor):
    wide_factor = factor[:, None, :]

    def forward_turn(turn_index, incoming):
        return passed_along(wide_factor * incoming + local_end, "ctx", 1)

    def backward_turn(turn_index, incoming):
        return passed_along(wide_factor * incoming + local_adjoint, "ctx", -1)

    entering = lax.fori_loop(0, lax.axis_size("ctx") - 1, forward_turn, jnp.zeros_like(local_end))
    arriving = lax.fori_loop(
        0, lax.axis_size("ctx") - 1, backward_turn, jnp.zeros_like(local_adjoint)
    )
    return (entering, arriving)


def local(projected, short_filter, residues, decay_rates, skip_gain, cotangent):
    batch_size = projected.shape[0]
    local_rows = projected.shape[1]
    channels = projected.shape[3]
    tap_count = short_filter.shape[1]
    filter_groups = residues.shape[0]
    group_width = channels // filter_groups
    previous = passed_along(projected[:, local_rows - (tap_count - 1) :], "ctx", 1)
    padded = jnp.concatenate([previous, projected], axis=1)
    mixed = short_conv(padded, short_filter, local_rows)
    query_part = mixed[:, :, 0]
    key_part = mixed[:, :, 1]
    value_part = mixed[:, :, 2]
    gated = key_part * value_part
    tables = block_tables(residues, decay_rates, BLK)
    carry_fwd, carry_bwd, decay_device = edge_tables(residues, decay_rates, local_rows)
    device_factor = decay_device.T
    block_shape = (batch_size, local_rows // BLK, BLK, group_width, filter_groups)
    conv_out, local_end = forward_local(gated.reshape(block_shape), tables)
    upstream = cotangent.astype(jnp.float32)
    grad_filtered = upstream * query_part
    conv_grad, local_adjoint = backward_local(grad_filtered.reshape(block_shape), tables)
    entering, arriving = chains(local_end, local_adjoint, device_factor)
    carried = jnp.einsum("gtn,bnwg->btwg", carry_fwd, entering, precision=HIGHEST)
    filtered = conv_out.reshape(gated.shape) + carried.reshape(gated.shape) + skip_gain * gated
    output = (query_part * filtered).astype(jnp.bfloat16)
    grad_query = upstream * filtered
    returned = jnp.einsum("gsn,bnwg->bswg", carry_bwd, arriving, precision=HIGHEST)
    grad_gated = (
        conv_grad.reshape(gated.shape) + returned.reshape(gated.shape) + skip_gain * grad_filtered
    )
    grad_mixed = jnp.stack([grad_query, grad_gated * value_part, grad_gated * key_part], axis=2)
    following = passed_along(grad_mixed[:, : tap_count - 1], "ctx", -1)
    ahead = jnp.concatenate([grad_mixed, following], axis=1)
    grad_projected = short_conv_grad(ahead, short_filter, local_rows).astype(jnp.bfloat16)
    short_local = filter_grad(grad_mixed, padded, tap_count, local_rows)
    skip_local = jnp.sum(grad_filtered * gated, axis=(0, 1))
    grad_short, grad_skip = lax.psum((short_local, skip_local), ("dp", "ctx"))
    return (output, grad_projected, grad_short, grad_skip)


def solution(mesh):
    placed = (P("dp", "ctx", None, None), P(), P(), P(), P(), P("dp", "ctx", None))
    return jax.shard_map(
        local,
        mesh=mesh,
        in_specs=placed,
        out_specs=(P("dp", "ctx", None), P("dp", "ctx", None, None), P(), P()),
        check_vma=False,
    )
```

profile of v0, /device:TPU:1, one launch (start us, length us, event | category | flops | bytes accessed | tf_op | source)
XLA Modules:
  0.0 1422.1 jit_solution(7022299706834155832)
XLA Ops:
  19.0 6.9 multiply_exponential_fusion
  25.9 7.2 rev.3
  33.3 16.8 %gather_fusion = f32[4096,512]{1,0:T(8,128)} fusion(f32[512,64]{0,1:T(8,128)S(1)} %copy.52, s32[4096]{0:T(1024)S(1)} %broadcast_clamp_fusion), kind=kCustom, calls=%fused_computation | custom fusion | bytes 16793600 | tf_op jit(solution)/shard_map/gather | solution.py:33
  50.1 16.2 %copy.53 = f32[64,64,512]{1,0,2:T(8,128)} copy(f32[64,64,512]{2,1,0:T(8,128)} %bitcast.190) | data formatting | bytes 16777216 | tf_op jit(solution)/shard_map/gather | solution.py:33
  66.9 18.8 %fusion.11 = f32[1,128,3,8192]{3,1,2,0:T(8,128)S(1)} fusion(bf16[1,128,3,8192]{3,1,2,0:T(8,128)(2,1)} %param.14, bf16[1,6,3,8192]{3,1,2,0:T(8,128)(2,1)S(1)} %collective-permute-done.2, f32[3,8192]{1,0:T(4,128)S(1)} %get-tuple-element.314, f32[3,8192]{1,0:T(4,128)S(1)} %get-tuple-element.315, f32[3,8192]{1,0:T(4,128)S(1)} %get-tuple-element.316, ...), kind=kLoop, calls=%fused_computation.38 | loop fusion | flops 119537664 | bytes 19857408 | tf_op jit(solution)/shard_map/add | solution.py:82
  92.0 9.1 copy.54
  101.1 13.1 fusion.67
  120.4 7.5 copy.59
  127.8 29.5 %fusion.2 = f32[512,2,16,64]{3,2,1,0:T(8,128)S(1)} fusion(f32[2,64,16,512]{1,2,0,3:T(8,128)} %copy.54, f32[64,64,512]{1,0,2:T(8,128)} %copy.53, pred[64,64]{1,0:T(8,128)(4,1)S(1)} %subtract_compare_fusion), kind=kOutput, calls=%fused_computation.9 | convolution fusion | flops 807403520 | bytes 16781312 | tf_op jit(solution)/shard_map/gts,bkswg->bktwg/dot_general | solution.py:40
  157.3 11.3 add_bitcast_fusion.1
  168.7 7.6 copy.60
  181.3 353.5 %while.50 = (s32[]{:T(128)}, f32[1,16,16,512]{3,2,1,0:T(8,128)S(1)}, f32[16,512]{1,0:T(8,128)S(1)}, f32[1,16,16,512]{3,2,1,0:T(8,128)S(1)}, s32[]{:T(128)}) while((s32[]{:T(128)}, f32[1,16,16,512]{3,2,1,0:T(8,128)S(1)}, f32[16,512]{1,0:T(8,128)S(1)}, f32[1,16,16,512]{3,2,1,0:T(8,128)S(1)}, s32[]{:T(128)}) %tuple.113), condition=%wide.region_4.5_spmd, body=%wide.region_3.4_spmd.sunk | while | flops 262146 | bytes 3702885 | solution.py:117
  496.8 6.5 collective-permute-start
  538.6 7.5 fusion.77
  555.1 13.5 multiply_reduce_fusion
  575.8 9.1 copy.66
  584.9 12.2 fusion.72
  597.1 19.1 %fusion = f32[512,2,16,64]{3,2,1,0:T(8,128)} fusion(f32[2,64,16,512]{1,2,0,3:T(8,128)S(1)} %copy-done.5, f32[64,64,512]{1,0,2:T(8,128)} %copy.53, pred[64,64]{1,0:T(8,128)(4,1)S(1)} %subtract_compare_fusion), kind=kOutput, calls=%fused_computation.7 | convolution fusion | flops 807403520 | bytes 16781312 | tf_op jit(solution)/shard_map/gts,bktwg->bkswg/dot_general | solution.py:57
  622.8 7.5 copy.69
  630.3 13.7 add_bitcast_fusion
  644.0 7.7 copy.70
  656.7 397.2 %while.51 = (s32[]{:T(128)}, f32[1,16,16,512]{3,2,1,0:T(8,128)S(1)}, f32[16,512]{1,0:T(8,128)S(1)}, f32[1,16,16,512]{3,2,1,0:T(8,128)S(1)}, s32[]{:T(128)}) while((s32[]{:T(128)}, f32[1,16,16,512]{3,2,1,0:T(8,128)S(1)}, f32[16,512]{1,0:T(8,128)S(1)}, f32[1,16,16,512]{3,2,1,0:T(8,128)S(1)}, s32[]{:T(128)}) %tuple.125), condition=%wide.region_8.9_spmd, body=%wide.region_7.8_spmd.sunk | while | flops 262146 | bytes 3702885 | solution.py:118
  658.8 11.4 collective-permute-done.1
  672.2 10.6 collective-permute-done.1
  684.8 11.4 collective-permute-done.1
  698.3 10.6 collective-permute-done.1
  710.9 11.4 collective-permute-done.1
  724.4 10.6 collective-permute-done.1
  737.0 11.4 collective-permute-done.1
  750.5 10.7 collective-permute-done.1
  763.2 10.7 collective-permute-done.1
  775.9 10.7 collective-permute-done.1
  788.7 10.7 collective-permute-done.1
  801.4 10.7 collective-permute-done.1
  814.1 10.7 collective-permute-done.1
  826.8 10.7 collective-permute-done.1
  839.6 10.7 collective-permute-done.1
  852.3 10.7 collective-permute-done.1
  865.0 10.7 collective-permute-done.1
  877.7 10.7 collective-permute-done.1
  890.5 10.7 collective-permute-done.1
  903.2 10.7 collective-permute-done.1
  915.9 10.7 collective-permute-done.1
  928.7 10.7 collective-permute-done.1
  941.4 10.7 collective-permute-done.1
  954.1 10.7 collective-permute-done.1
  966.8 10.7 collective-permute-done.1
  979.6 10.7 collective-permute-done.1
  992.3 10.7 collective-permute-done.1
  1005.0 10.7 collective-permute-done.1
  1017.7 10.7 collective-permute-done.1
  1030.5 10.7 collective-permute-done.1
  1043.2 10.7 collective-permute-done.1
  1057.7 7.5 fusion.80
  1074.3 10.8 fusion.51
  1085.1 9.8 fusion.52
  1094.9 10.9 fusion.13
  1105.8 9.3 pad_maximum_fusion.1
  1119.3 11.2 fusion.15
  1157.5 27.9 %reduce_sum.28 = f32[3,7,8192]{2,0,1:T(4,128)} reduce(f32[1,128,3,7,8192]{4,1,2,3,0:T(8,128)} %fusion.25, f32[]{:T(128)} %constant.65.clone.1), dimensions={0,1}, to_apply=%region_9.10 | reduce | flops 21848064 | bytes 88768512 | tf_op jit(solution)/shard_map/reduce_sum | solution.py:105
  1185.5 102.3 %psum.15 = f32[8192]{0:T(1024)} all-reduce(f32[8192]{0:T(1024)S(1)} %copy-done.25), channel_id=1, replica_groups=mesh['dp'=4,'ctx'=32] {'dp','ctx'}, use_global_device_ids=true, to_apply=%region_12.13 | all-reduce | flops 8192 | bytes 65536 | tf_op jit(solution)/shard_map/psum | solution.py:161
  1287.8 80.9 %all-reduce.2.cloned.1.call-done = f32[3,7,8192]{2,0,1:T(4,128)} async-done(((f32[3,7,8192]{2,0,1:T(4,128)}), f32[3,7,8192]{2,0,1:T(4,128)}) %all-reduce.2.cloned.1.call-update) | async-done | bytes 688144 | tf_op jit(solution)/shard_map/psum | solution.py:161
  1371.6 9.8 pad_maximum_fusion
  1381.5 33.6 %fusion.27 = bf16[1,128,3,8192]{3,1,2,0:T(8,128)(2,1)} fusion(f32[1,134,3,8192]{3,1,2,0:T(8,128)} %pad_maximum_fusion, f32[3,8192]{1,0:T(4,128)S(1)} %copy-done.13, f32[3,8192]{1,0:T(4,128)S(1)} %copy-done.15, f32[3,8192]{1,0:T(4,128)S(1)} %copy-done.17, f32[3,8192]{1,0:T(4,128)S(1)} %copy-done.19, f32[3,8192]{1,0:T(4,128)S(1)} %copy-done.21, ...), kind=kLoop, calls=%fused_computation.55 | loop fusion | flops 50331648 | bytes 95059968 | tf_op jit(solution)/shard_map/convert_element_type | solution.py:158
  (274 shorter events, 518.5 us)
Async XLA Ops:
  7.2 1361.6 %all-reduce.2.cloned.1.call-start = ((), (), s32[]{:S(2)}) async-start(), calls=%async_computation | async-start | bytes 1835008 | tf_op jit(solution)/shard_map/psum | solution.py:161
  8.3 58.6 %collective-permute-start.2 = (bf16[1,6,3,8192]{3,1,2,0:T(8,128)(2,1)S(1)}, bf16[1,6,3,8192]{3,1,2,0:T(8,128)(2,1)S(1)}, u32[]{:S(2)}, u32[]{:S(2)}) collective-permute-start(bf16[1,6,3,8192]{3,1,2,0:T(8,128)(2,1)S(1)} %slice.87), channel_id=1, source_target_pairs={{0,1},{1,2},{2,3},{3,4},{4,5},{5,6},{6,7},{7,8},{8,9},{9,10},{10,1... | collective-permute-start | bytes 884744 | tf_op jit(solution)/shard_map/ppermute | solution.py:13
  189.6 10.5 collective-permute-start
  200.2 10.5 collective-permute-start
  210.8 10.5 collective-permute-start
  221.4 10.5 collective-permute-start
  232.1 10.5 collective-permute-start
  242.7 10.5 collective-permute-start
  253.3 10.5 collective-permute-start
  263.9 10.5 collective-permute-start
  274.5 10.5 collective-permute-start
  285.1 10.5 collective-permute-start
  295.8 10.5 collective-permute-start
  306.4 10.5 collective-permute-start
  317.0 10.5 collective-permute-start
  327.6 10.5 collective-permute-start
  338.2 10.5 collective-permute-start
  348.9 10.5 collective-permute-start
  359.5 10.5 collective-permute-start
  370.1 12.0 collective-permute-start
  382.2 12.6 collective-permute-start
  395.0 12.6 collective-permute-start
  407.7 12.6 collective-permute-start
  420.4 12.6 collective-permute-start
  433.1 12.6 collective-permute-start
  445.9 12.6 collective-permute-start
  458.6 12.6 collective-permute-start
  471.3 12.6 collective-permute-start
  484.1 12.6 collective-permute-start
  496.8 12.6 collective-permute-start
  509.5 12.6 collective-permute-start
  522.2 12.6 collective-permute-start
  656.8 13.4 collective-permute-start.1
  670.3 12.5 collective-permute-start.1
  682.9 13.4 collective-permute-start.1
  696.4 12.5 collective-permute-start.1
  709.0 13.4 collective-permute-start.1
  722.5 12.5 collective-permute-start.1
  735.1 13.4 collective-permute-start.1
  748.5 12.6 collective-permute-start.1
  761.3 12.6 collective-permute-start.1
  774.0 12.6 collective-permute-start.1
  786.7 12.6 collective-permute-start.1
  799.5 12.6 collective-permute-start.1
  812.2 12.6 collective-permute-start.1
  824.9 12.6 collective-permute-start.1
  837.6 12.6 collective-permute-start.1
  850.4 12.6 collective-permute-start.1
  863.1 12.6 collective-permute-start.1
  875.8 12.6 collective-permute-start.1
  888.5 12.6 collective-permute-start.1
  901.3 12.6 collective-permute-start.1
  914.0 12.6 collective-permute-start.1
  926.7 12.6 collective-permute-start.1
  939.5 12.6 collective-permute-start.1
  952.2 12.6 collective-permute-start.1
  964.9 12.6 collective-permute-start.1
  977.6 12.6 collective-permute-start.1
  990.4 12.6 collective-permute-start.1
  1003.1 12.6 collective-permute-start.1
  1015.8 12.6 collective-permute-start.1
  1028.5 12.6 collective-permute-start.1
  1041.3 12.6 collective-permute-start.1
  1117.0 254.2 %collective-permute-start.3 = (f32[1,6,3,8192]{3,0,2,1:T(1,128)S(1)}, f32[1,6,3,8192]{3,0,2,1:T(1,128)S(1)}, u32[]{:S(2)}, u32[]{:S(2)}) collective-permute-start(f32[1,6,3,8192]{3,0,2,1:T(1,128)S(1)} %copy.74), channel_id=1, source_target_pairs={{1,0},{2,1},{3,2},{4,3},{5,4},{6,5},{7,6},{8,7},{9,8},{10,9},{11,1... | collective-permute-start | bytes 1769480 | tf_op jit(solution)/shard_map/ppermute | solution.py:13
  (29 other events, 431.1 us)
Sparse Core Ops, SparseCore 0:
  1185.6 183.0 all-reduce.1
where the time goes:
time: 1430 us; the launch traced here: 1420 us
  waiting for transfers between devices  604 us (42%)
  starting transfers between devices  227 us (16%)
  other arithmetic  199 us (14%)
  local copies, waits for them, and re-layouts  160 us (11%)
  matrix products  114 us (8%)
  blocking collectives  102 us (7%)
  between operations  14.9 us (1%)
    ppermute x64, waiting for transfers between devices, passed_along(): lax.ppermute(value, axis, [(source, source + steps) for source in range(f...  523 us
    ppermute x64, starting transfers between devices, passed_along(): lax.ppermute(value, axis, [(source, source + steps) for source in range(f...  227 us
    psum x1, blocking collectives, local(): grad_short, grad_skip = lax.psum((short_local, skip_local), ('dp', 'ctx'))  102 us
    psum x1, waiting for transfers between devices, local(): grad_short, grad_skip = lax.psum((short_local, skip_local), ('dp', 'ctx'))  80.9 us
    unnamed x9, other arithmetic  43.6 us
    convert_element_type x1, other arithmetic, local(): short_conv_grad(ahead, short_filter, local_rows).astype(jnp.bfloat16)  33.6 us
    gather x2, local copies, waits for them, and re-layouts, block_tables(): lag_filter[:, jnp.maximum(lag_index, 0)]  33.1 us
    another operation x9, local copies, waits for them, and re-layouts  32 us
  transfers between devices with their start and end apart: 65, of which 63 were waited for; matrix products, arithmetic and copies ran while one was open for 9% of the time, Pallas kernels for 0%

commit v1 on v0

--- a/solution.py
+++ b/solution.py
@@ -158,7 +158,9 @@
     grad_projected = short_conv_grad(ahead, short_filter, local_rows).astype(jnp.bfloat16)
     short_local = filter_grad(grad_mixed, padded, tap_count, local_rows)
     skip_local = jnp.sum(grad_filtered * gated, axis=(0, 1))
-    grad_short, grad_skip = lax.psum((short_local, skip_local), ("dp", "ctx"))
+    grad_short, grad_skip = jax.lax.psum(
+        jax.lax.psum((short_local, skip_local), "ctx"), axis_name="dp"
+    )
     return (output, grad_projected, grad_short, grad_skip)
 
 

time: 1430 us -> 1420 us (level)
  waiting for transfers between devices: 604 us -> 525 us
  blocking collectives: 102 us -> 157 us
    psum x1 -> x2, waiting for transfers between devices: 80.9 us -> 2.56 us  [the longest x1 2.56 us: local(): jax.lax.psum(jax.lax.psum((short_local, skip_local), 'ctx'), axis_name='dp')]
    psum x1 -> x2, blocking collectives: 102 us -> 157 us  [the longest x1 142 us: local(): jax.lax.psum((short_local, skip_local), 'ctx')]
  transfers between devices with their start and end apart: 65 -> 66, of which waited for: 63 -> 63; matrix products, arithmetic and copies ran while one was open for 9% -> 12% of each run, Pallas kernels for 0% -> 0%
where the time goes in v1:
time: 1420 us; the launch traced here: 1400 us
  waiting for transfers between devices  525 us (37%)
  starting transfers between devices  227 us (16%)
  other arithmetic  200 us (14%)
  local copies, waits for them, and re-layouts  160 us (11%)
  blocking collectives  157 us (11%)
  matrix products  114 us (8%)
  between operations  15.2 us (1%)
    ppermute x64, waiting for transfers between devices, passed_along(): lax.ppermute(value, axis, [(source, source + steps) for source in range(f...  523 us
    ppermute x64, starting transfers between devices, passed_along(): lax.ppermute(value, axis, [(source, source + steps) for source in range(f...  227 us
    psum x1, blocking collectives, local(): jax.lax.psum((short_local, skip_local), 'ctx')  142 us
    unnamed x9, other arithmetic  44.1 us
    convert_element_type x1, other arithmetic, local(): short_conv_grad(ahead, short_filter, local_rows).astype(jnp.bfloat16)  34.2 us
    gather x2, local copies, waits for them, and re-layouts, block_tables(): lag_filter[:, jnp.maximum(lag_index, 0)]  33.2 us
    another operation x9, local copies, waits for them, and re-layouts  32 us
    another operation x3, other arithmetic, local(): jnp.stack([grad_query, grad_gated * value_part, grad_gated * key_part], a...  30 us
  transfers between devices with their start and end apart: 66, of which 63 were waited for; matrix products, arithmetic and copies ran while one was open for 12% of the time, Pallas kernels for 0%

profile of v1, /device:TPU:1, one launch (start us, length us, event | category | flops | bytes accessed | tf_op | source)
XLA Modules:
  0.0 1399.7 jit_solution(12196109264308850510)
XLA Ops:
  19.0 6.9 multiply_exponential_fusion
  25.9 7.2 rev.3
  33.3 16.9 %gather_fusion = f32[4096,512]{1,0:T(8,128)} fusion(f32[512,64]{0,1:T(8,128)S(1)} %copy.52, s32[4096]{0:T(1024)S(1)} %broadcast_clamp_fusion), kind=kCustom, calls=%fused_computation | custom fusion | bytes 16793600 | tf_op jit(solution)/shard_map/gather | solution.py:33
  50.2 16.3 %copy.53 = f32[64,64,512]{1,0,2:T(8,128)} copy(f32[64,64,512]{2,1,0:T(8,128)} %bitcast.190) | data formatting | bytes 16777216 | tf_op jit(solution)/shard_map/gather | solution.py:33
  67.0 18.8 %fusion.11 = f32[1,128,3,8192]{3,1,2,0:T(8,128)S(1)} fusion(bf16[1,128,3,8192]{3,1,2,0:T(8,128)(2,1)} %param.14, bf16[1,6,3,8192]{3,1,2,0:T(8,128)(2,1)S(1)} %collective-permute-done.2, f32[3,8192]{1,0:T(4,128)S(1)} %get-tuple-element.314, f32[3,8192]{1,0:T(4,128)S(1)} %get-tuple-element.315, f32[3,8192]{1,0:T(4,128)S(1)} %get-tuple-element.316, ...), kind=kLoop, calls=%fused_computation.38 | loop fusion | flops 119537664 | bytes 19857408 | tf_op jit(solution)/shard_map/add | solution.py:82
  92.1 9.1 copy.54
  101.2 12.9 fusion.67
  120.2 7.5 copy.59
  127.7 29.5 %fusion.2 = f32[512,2,16,64]{3,2,1,0:T(8,128)S(1)} fusion(f32[2,64,16,512]{1,2,0,3:T(8,128)} %copy.54, f32[64,64,512]{1,0,2:T(8,128)} %copy.53, pred[64,64]{1,0:T(8,128)(4,1)S(1)} %subtract_compare_fusion), kind=kOutput, calls=%fused_computation.9 | convolution fusion | flops 807403520 | bytes 16781312 | tf_op jit(solution)/shard_map/gts,bkswg->bktwg/dot_general | solution.py:40
  157.2 11.6 add_bitcast_fusion.1
  168.7 7.6 copy.60
  181.4 353.5 %while.50 = (s32[]{:T(128)}, f32[1,16,16,512]{3,2,1,0:T(8,128)S(1)}, f32[16,512]{1,0:T(8,128)S(1)}, f32[1,16,16,512]{3,2,1,0:T(8,128)S(1)}, s32[]{:T(128)}) while((s32[]{:T(128)}, f32[1,16,16,512]{3,2,1,0:T(8,128)S(1)}, f32[16,512]{1,0:T(8,128)S(1)}, f32[1,16,16,512]{3,2,1,0:T(8,128)S(1)}, s32[]{:T(128)}) %tuple.113), condition=%wide.region_4.5_spmd, body=%wide.region_3.4_spmd.sunk | while | flops 262146 | bytes 3702885 | solution.py:117
  496.9 6.5 collective-permute-start
  538.7 7.5 fusion.77
  555.1 13.5 multiply_reduce_fusion
  575.8 9.1 copy.66
  584.9 12.2 fusion.72
  597.2 19.1 %fusion = f32[512,2,16,64]{3,2,1,0:T(8,128)} fusion(f32[2,64,16,512]{1,2,0,3:T(8,128)S(1)} %copy-done.5, f32[64,64,512]{1,0,2:T(8,128)} %copy.53, pred[64,64]{1,0:T(8,128)(4,1)S(1)} %subtract_compare_fusion), kind=kOutput, calls=%fused_computation.7 | convolution fusion | flops 807403520 | bytes 16781312 | tf_op jit(solution)/shard_map/gts,bktwg->bkswg/dot_general | solution.py:57
  622.6 7.5 copy.69
  630.2 13.7 add_bitcast_fusion
  643.9 7.7 copy.70
  656.6 397.2 %while.51 = (s32[]{:T(128)}, f32[1,16,16,512]{3,2,1,0:T(8,128)S(1)}, f32[16,512]{1,0:T(8,128)S(1)}, f32[1,16,16,512]{3,2,1,0:T(8,128)S(1)}, s32[]{:T(128)}) while((s32[]{:T(128)}, f32[1,16,16,512]{3,2,1,0:T(8,128)S(1)}, f32[16,512]{1,0:T(8,128)S(1)}, f32[1,16,16,512]{3,2,1,0:T(8,128)S(1)}, s32[]{:T(128)}) %tuple.127), condition=%wide.region_8.9_spmd, body=%wide.region_7.8_spmd.sunk | while | flops 262146 | bytes 3702885 | solution.py:118
  658.6 11.4 collective-permute-done.1
  672.1 10.6 collective-permute-done.1
  684.7 11.4 collective-permute-done.1
  698.2 10.6 collective-permute-done.1
  710.8 11.4 collective-permute-done.1
  724.3 10.6 collective-permute-done.1
  736.9 11.4 collective-permute-done.1
  750.3 10.7 collective-permute-done.1
  763.1 10.7 collective-permute-done.1
  775.8 10.7 collective-permute-done.1
  788.5 10.7 collective-permute-done.1
  801.3 10.7 collective-permute-done.1
  814.0 10.7 collective-permute-done.1
  826.7 10.7 collective-permute-done.1
  839.4 10.7 collective-permute-done.1
  852.2 10.7 collective-permute-done.1
  864.9 10.7 collective-permute-done.1
  877.6 10.7 collective-permute-done.1
  890.4 10.7 collective-permute-done.1
  903.1 10.7 collective-permute-done.1
  915.8 10.7 collective-permute-done.1
  928.5 10.7 collective-permute-done.1
  941.3 10.7 collective-permute-done.1
  954.0 10.7 collective-permute-done.1
  966.7 10.7 collective-permute-done.1
  979.4 10.7 collective-permute-done.1
  992.2 10.7 collective-permute-done.1
  1004.9 10.7 collective-permute-done.1
  1017.6 10.7 collective-permute-done.1
  1030.4 10.7 collective-permute-done.1
  1043.1 10.7 collective-permute-done.1
  1057.6 7.5 fusion.80
  1074.2 10.8 fusion.51
  1085.0 9.8 fusion.52
  1094.9 10.9 fusion.13
  1105.8 9.3 pad_maximum_fusion.1
  1119.3 11.2 fusion.15
  1158.0 27.9 %reduce_sum.28 = f32[3,7,8192]{2,0,1:T(4,128)} reduce(f32[1,128,3,7,8192]{4,1,2,3,0:T(8,128)} %fusion.25, f32[]{:T(128)} %constant.65.clone.1), dimensions={0,1}, to_apply=%region_9.10 | reduce | flops 21848064 | bytes 88768512 | tf_op jit(solution)/shard_map/reduce_sum | solution.py:105
  1186.0 142.0 %psum.30 = f32[8192]{0:T(1024)S(1)} all-reduce(f32[8192]{0:T(1024)S(1)} %copy-done.25), channel_id=1, replica_groups=mesh['dp'=4,'ctx'=32] {'ctx'}, use_global_device_ids=true, to_apply=%region_13.14 | all-reduce | flops 8192 | bytes 65536 | tf_op jit(solution)/shard_map/psum | solution.py:162
  1328.1 14.7 %psum.31 = f32[8192]{0:T(1024)} all-reduce(f32[8192]{0:T(1024)S(1)} %psum.30), channel_id=1, replica_groups=mesh['dp'=4,'ctx'=32] {'dp'}, use_global_device_ids=true, to_apply=%region_14.15 | all-reduce | flops 8192 | bytes 65536 | tf_op jit(solution)/shard_map/psum | solution.py:161
  1343.2 9.8 pad_maximum_fusion
  1353.1 34.2 %fusion.27 = bf16[1,128,3,8192]{3,1,2,0:T(8,128)(2,1)} fusion(f32[1,134,3,8192]{3,1,2,0:T(8,128)} %pad_maximum_fusion, f32[3,8192]{1,0:T(4,128)S(1)} %copy-done.13, f32[3,8192]{1,0:T(4,128)S(1)} %copy-done.15, f32[3,8192]{1,0:T(4,128)S(1)} %copy-done.17, f32[3,8192]{1,0:T(4,128)S(1)} %copy-done.19, f32[3,8192]{1,0:T(4,128)S(1)} %copy-done.21, ...), kind=kLoop, calls=%fused_computation.55 | loop fusion | flops 50331648 | bytes 95059968 | tf_op jit(solution)/shard_map/convert_element_type | solution.py:158
  (278 shorter events, 521.4 us)
Async XLA Ops:
  7.2 1335.6 %all-reduce.3.cloned.1.call-start = ((), (), s32[]{:S(2)}) async-start(), calls=%async_computation | async-start | bytes 1835008 | tf_op jit(solution)/shard_map/psum | solution.py:162
  8.3 58.7 %collective-permute-start.2 = (bf16[1,6,3,8192]{3,1,2,0:T(8,128)(2,1)S(1)}, bf16[1,6,3,8192]{3,1,2,0:T(8,128)(2,1)S(1)}, u32[]{:S(2)}, u32[]{:S(2)}) collective-permute-start(bf16[1,6,3,8192]{3,1,2,0:T(8,128)(2,1)S(1)} %slice.87), channel_id=1, source_target_pairs={{0,1},{1,2},{2,3},{3,4},{4,5},{5,6},{6,7},{7,8},{8,9},{9,10},{10,1... | collective-permute-start | bytes 884744 | tf_op jit(solution)/shard_map/ppermute | solution.py:13
  189.7 10.5 collective-permute-start
  200.3 10.5 collective-permute-start
  210.9 10.5 collective-permute-start
  221.5 10.5 collective-permute-start
  232.1 10.5 collective-permute-start
  242.8 10.5 collective-permute-start
  253.4 10.5 collective-permute-start
  264.0 10.5 collective-permute-start
  274.6 10.5 collective-permute-start
  285.2 10.5 collective-permute-start
  295.9 10.5 collective-permute-start
  306.5 10.5 collective-permute-start
  317.1 10.5 collective-permute-start
  327.7 10.5 collective-permute-start
  338.3 10.5 collective-permute-start
  348.9 10.5 collective-permute-start
  370.2 12.0 collective-permute-start
  382.3 12.6 collective-permute-start
  395.1 12.6 collective-permute-start
  407.8 12.6 collective-permute-start
  420.5 12.6 collective-permute-start
  433.2 12.6 collective-permute-start
  446.0 12.6 collective-permute-start
  458.7 12.6 collective-permute-start
  471.4 12.6 collective-permute-start
  484.1 12.6 collective-permute-start
  496.9 12.6 collective-permute-start
  509.6 12.6 collective-permute-start
  522.3 12.6 collective-permute-start
  656.7 13.4 collective-permute-start.1
  670.2 12.5 collective-permute-start.1
  682.8 13.4 collective-permute-start.1
  696.3 12.5 collective-permute-start.1
  708.9 13.4 collective-permute-start.1
  722.3 12.5 collective-permute-start.1
  734.9 13.4 collective-permute-start.1
  748.4 12.6 collective-permute-start.1
  761.1 12.6 collective-permute-start.1
  773.9 12.6 collective-permute-start.1
  786.6 12.6 collective-permute-start.1
  799.3 12.6 collective-permute-start.1
  812.1 12.6 collective-permute-start.1
  824.8 12.6 collective-permute-start.1
  837.5 12.6 collective-permute-start.1
  850.2 12.6 collective-permute-start.1
  863.0 12.6 collective-permute-start.1
  875.7 12.6 collective-permute-start.1
  888.4 12.6 collective-permute-start.1
  901.1 12.6 collective-permute-start.1
  913.9 12.6 collective-permute-start.1
  926.6 12.6 collective-permute-start.1
  939.3 12.6 collective-permute-start.1
  952.1 12.6 collective-permute-start.1
  964.8 12.6 collective-permute-start.1
  977.5 12.6 collective-permute-start.1
  990.2 12.6 collective-permute-start.1
  1003.0 12.6 collective-permute-start.1
  1015.7 12.6 collective-permute-start.1
  1028.4 12.6 collective-permute-start.1
  1041.1 12.6 collective-permute-start.1
  1117.0 225.8 %collective-permute-start.3 = (f32[1,6,3,8192]{3,0,2,1:T(1,128)S(1)}, f32[1,6,3,8192]{3,0,2,1:T(1,128)S(1)}, u32[]{:S(2)}, u32[]{:S(2)}) collective-permute-start(f32[1,6,3,8192]{3,0,2,1:T(1,128)S(1)} %copy.74), channel_id=1, source_target_pairs={{1,0},{2,1},{3,2},{4,3},{5,4},{6,5},{7,6},{8,7},{9,8},{10,9},{11,1... | collective-permute-start | bytes 1769480 | tf_op jit(solution)/shard_map/ppermute | solution.py:13
  1186.0 203.9 %all-reduce.5.cloned.1.call-start = ((), (), s32[]{:S(2)}) async-start(), calls=%async_computation.1 | async-start | bytes 1835008 | tf_op jit(solution)/shard_map/psum | solution.py:161
  (30 other events, 442.1 us)
Sparse Core Ops, SparseCore 0:
  1186.1 140.2 all-reduce.2
  1342.9 46.9 all-reduce.4
